TPU v7x, 32 devices: a whole 2x2x4 slice. The times are simulated.
32 devices in a mesh: video: 4 (over x, core), frame: 8 (over z, y).
Axes of the slice: x: 2, y: 2, z: 4, core: 2. Of those that a mesh axis runs over, the one named last changes fastest.
Arguments:
- frames: bfloat16 [32, 1024, 640], P(('video', 'frame')), parts along dimension 0, may hold values from -6 to 6
- ref_rows: bfloat16 [4096, 640], P(('video', 'frame')), parts along dimension 0, may hold values from -6 to 6
- w_query: bfloat16 [640, 640], replicated, may hold values from -1 to 1
- w_key: bfloat16 [640, 640], replicated, may hold values from -1 to 1
- w_value: bfloat16 [640, 640], replicated, may hold values from -0.25 to 0.25
- w_out: bfloat16 [640, 640], replicated, may hold values from -0.25 to 0.25
- w_conv: bfloat16 [3, 640, 640], replicated, may hold values from -0.125 to 0.125
- t_query: bfloat16 [640, 640], replicated, may hold values from -1 to 1
- t_key: bfloat16 [640, 640], replicated, may hold values from -1 to 1
- t_value: bfloat16 [640, 640], replicated, may hold values from -0.25 to 0.25
- t_out: bfloat16 [640, 640], replicated, may hold values from -0.25 to 0.25
Outputs:
- result: bfloat16 [32, 1024, 640], P(('video', 'frame')), parts along dimension 0
There are 4 independent parts, one for each index of `video`. A program takes and returns all parts, laid end to end along the dimension named above; an argument that names none is the same for every part. Nothing has to cross between parts.
All inputs are finite; a program needn't handle non-finite values.
Results may differ from a plain program's by a relative error of at most 0.011.
Values may be sent and summed in bfloat16 or wider, within the bound.
A program may use at most 128 MiB of HBM per device.

v0:
```python
import math
import jax
import jax.numpy as jnp
from jax import lax
from jax.sharding import PartitionSpec as P

HEADS = 10


def padded_2(value, sides, width):
    for axis, dim in sides:
        devices, length = (lax.axis_size(axis), value.shape[dim])
        up = [(i, (i + 1) % devices) for i in range(devices - 1)]
        down = [(j, i) for i, j in up]
        last = lax.slice_in_dim(value, length - width, length, axis=dim)
        leading = lax.slice_in_dim(value, 0, width, axis=dim)
        before = lax.ppermute(last, axis, up)
        after = lax.ppermute(leading, axis, down)
        value = jnp.concatenate([before, value, after], axis=dim)
    return value


def layer_norm(value):
    mean = jnp.mean(value, axis=-1, keepdims=True)
    centered = value - mean
    var = jnp.mean(centered * centered, axis=-1, keepdims=True)
    return centered * lax.rsqrt(var + 1e-05)


def project(rows, weight):
    return jnp.dot(rows, weight, preferred_element_type=jnp.float32).astype(jnp.bfloat16)


def split_heads(value, heads):
    nframes, pixels, width = value.shape
    return value.reshape(nframes, pixels, heads, width // heads).transpose(2, 0, 1, 3)


def temporal_attend(tquery, tkeys, tvalues):
    nframes, pixels, width = tquery.shape
    head_dim = width // HEADS
    shaped_q = tquery.reshape(nframes, pixels, HEADS, head_dim)
    shaped_k = tkeys.reshape(nframes, pixels, HEADS, head_dim)
    shaped_v = tvalues.reshape(nframes, pixels, HEADS, head_dim)
    tscores = jnp.einsum(
        "fnhd,gnhd->nhfg", shaped_q, shaped_k, preferred_element_type=jnp.float32
    ) / math.sqrt(head_dim)
    tpeak = jnp.max(tscores, axis=-1, keepdims=True)
    texpo = jnp.exp(tscores - tpeak)
    ttotal = jnp.sum(texpo, axis=-1)
    tmixed = (
        jnp.einsum(
            "nhfg,gnhd->nhfd",
            texpo.astype(jnp.bfloat16),
            shaped_v,
            preferred_element_type=jnp.float32,
        )
        / ttotal[..., None]
    )
    return tmixed.transpose(2, 0, 1, 3).reshape(nframes, pixels, width).astype(jnp.bfloat16)


def per_device(
    frames, ref_rows, w_query, w_key, w_value, w_out, w_conv, t_query, t_key, t_value, t_out
):
    fdev, pixels, width = frames.shape
    head_dim = width // HEADS
    scale = 1.0 / math.sqrt(head_dim)
    ndev = lax.axis_size("frame")
    group_px = pixels // ndev
    normed = layer_norm(frames.astype(jnp.float32)).astype(jnp.bfloat16).reshape(-1, width)
    query = split_heads(project(normed, w_query).reshape(fdev, pixels, width), HEADS)
    keys = split_heads(project(normed, w_key).reshape(fdev, pixels, width), HEADS)
    values = split_heads(project(normed, w_value).reshape(fdev, pixels, width), HEADS)

    def local_part(args):
        qa, ka, va = args
        scores = jnp.einsum("fqd,fkd->fqk", qa, ka, preferred_element_type=jnp.float32) * scale
        peak = jnp.max(scores, axis=-1)
        expo = jnp.exp(scores - peak[..., None])
        total = jnp.sum(expo, axis=-1)
        accum = jnp.einsum(
            "fqk,fkd->fqd", expo.astype(jnp.bfloat16), va, preferred_element_type=jnp.float32
        )
        return (peak, total, accum)

    start_carry = lax.map(local_part, (query, keys, values))
    ref_keys = project(ref_rows, w_key)
    ref_values = project(ref_rows, w_value)
    piece_keys = lax.all_gather(ref_keys, "frame", axis=0, tiled=True)
    piece_values = lax.all_gather(ref_values, "frame", axis=0, tiled=True)
    count = piece_keys.shape[0]
    heads_k = piece_keys.reshape(count, HEADS, head_dim).transpose(1, 0, 2)
    heads_v = piece_values.reshape(count, HEADS, head_dim).transpose(1, 0, 2)

    def one_head(args):
        qa, peak, total, accum, ka, va = args
        scores = jnp.einsum("fqd,kd->fqk", qa, ka, preferred_element_type=jnp.float32) * scale
        newpeak = jnp.maximum(peak, jnp.max(scores, axis=-1))
        factor = jnp.exp(peak - newpeak)
        expo = jnp.exp(scores - newpeak[..., None])
        total = total * factor + jnp.sum(expo, axis=-1)
        accum = accum * factor[..., None] + jnp.einsum(
            "fqk,kd->fqd", expo.astype(jnp.bfloat16), va, preferred_element_type=jnp.float32
        )
        return (newpeak, total, accum)

    final = lax.map(
        one_head, (query, start_carry[0], start_carry[1], start_carry[2], heads_k, heads_v)
    )
    attended = (
        (final[2] / final[1][..., None])
        .transpose(1, 2, 0, 3)
        .reshape(-1, width)
        .astype(jnp.bfloat16)
    )
    first = (
        frames.astype(jnp.float32)
        + jnp.dot(attended, w_out, preferred_element_type=jnp.float32).reshape(fdev, pixels, width)
    ).astype(jnp.bfloat16)
    padded = padded_2(first, (("frame", 0),), 1)
    conv = jnp.zeros((fdev * pixels, width), jnp.float32)
    for tap in range(3):
        conv = conv + jnp.dot(
            padded[tap : tap + fdev].reshape(-1, width),
            w_conv[tap],
            preferred_element_type=jnp.float32,
        )
    second = (first.astype(jnp.float32) + conv.reshape(fdev, pixels, width)).astype(jnp.bfloat16)
    normed2 = layer_norm(second.astype(jnp.float32)).astype(jnp.bfloat16)
    grouped = normed2.reshape(fdev, ndev, group_px, width)
    features = lax.all_to_all(grouped, "frame", split_axis=1, concat_axis=0, tiled=True)
    nframes, groups, count, channels = features.shape
    flat = features.reshape(-1, channels)
    tquery = project(flat, t_query).reshape(nframes, groups * count, channels)
    tkeys = project(flat, t_key).reshape(nframes, groups * count, channels)
    tvalues = project(flat, t_value).reshape(nframes, groups * count, channels)
    mixed = temporal_attend(tquery, tkeys, tvalues).reshape(nframes, groups, count, channels)
    back = lax.all_to_all(mixed, "frame", split_axis=0, concat_axis=1, tiled=True)
    result = second.astype(jnp.float32) + jnp.dot(
        back.reshape(-1, width), t_out, preferred_element_type=jnp.float32
    ).reshape(fdev, pixels, width)
    return result.astype(jnp.bfloat16)


def solution(mesh):
    return jax.shard_map(
        per_device,
        mesh=mesh,
        in_specs=(
            P(("video", "frame"), None, None),
            P(("video", "frame"), None),
            P(),
            P(),
            P(),
            P(),
            P(),
            P(),
            P(),
            P(),
            P(),
        ),
        out_specs=P(("video", "frame"), None, None),
        check_vma=False,
    )
```

profile of v0, /device:TPU:0, one launch (start us, length us, event | category | flops | bytes accessed | tf_op | source)
XLA Modules:
  0.0 356.0 jit_solution(769306988038147561)
XLA Ops:
  15.3 2.6 convolution_convert_fusion.3
  20.4 3.5 copy.52
  24.0 3.8 %copy.53 = bf16[1,1024,10,64]{3,1,0,2:T(8,128)(2,1)} copy(bf16[1,1024,10,64]{1,3,2,0:T(8,128)(2,1)} %bitcast.198) | data formatting | bytes 2621440 | tf_op jit(solution)/shard_map/reshape;reshape | solution.py:36
  27.8 3.8 %copy.54 = bf16[1,1024,10,64]{3,1,0,2:T(8,128)(2,1)} copy(bf16[1,1024,10,64]{1,3,2,0:T(8,128)(2,1)} %bitcast.197) | data formatting | bytes 2621440 | tf_op jit(solution)/shard_map/reshape;reshape | solution.py:36
  33.4 49.6 %while.26 = (s32[]{:T(128)}, f32[10,1,1024]{2,1,0:T(1,128)S(1)}, f32[10,1,1024]{2,1,0:T(1,128)S(1)}, f32[10,1,1024,64]{2,3,1,0:T(8,128)}, bf16[10,1,1024,64]{3,2...) while((s32[]{:T(128)}, f32[10,1,1024]{2,1,0:T(1,128)S(1)}, ...), condition=%wide.region_5.6_spmd, body=%wide.region_2.5_spmd.sunk | while | flops 276822016 | bytes 13666393 | solution.py:87
  85.5 11.4 %all-gather.5.cloned.1.call-done = bf16[1024,640]{1,0:T(8,128)(2,1)} async-done(((bf16[128,640]{1,0:T(8,128)(2,1)}), bf16[1024,640]{1,0:T(8,128)(2,1)}) %all-gather.5.cloned.1.call-update) | async-done | bytes 1310736 | tf_op jit(solution)/shard_map/all_gather | solution.py:91
  101.2 51.8 %while.27 = (s32[]{:T(128)}, f32[10,1,1024]{2,0,1:T(8,128)S(1)}, f32[10,1,1024,64]{2,3,1,0:T(8,128)}, f32[10,1,1024]{2,1,0:T(1,128)S(1)}, f32[10,1,1024]{2,1,0:T...) while((s32[]{:T(128)}, f32[10,1,1024]{2,0,1:T(8,128)S(1)}, ...), condition=%wide.region_9.10_spmd, body=%wide.region_6.9_spmd.sunk | while | flops 276959232 | bytes 13707385 | solution.py:108
  118.4 2.6 fusion.119
  123.6 2.6 fusion.119
  128.8 2.6 fusion.119
  134.0 2.6 fusion.119
  139.1 2.6 fusion.119
  144.3 2.6 fusion.119
  149.5 2.6 fusion.119
  162.1 51.6 %collective-permute-done = bf16[1,1024,640]{2,1,0:T(8,128)(2,1)S(1)} collective-permute-done((bf16[1,1024,640]{2,1,0:T(8,128)(2,1)S(1)}, bf16[1,1024,640]{2,1,0:T(8,128)(2,1)S(1)}, u32[]{:S(2)}, u32[]{:S(2)}) %collective-permute-start) | collective-permute-done | bytes 1310752 | tf_op jit(solution)/shard_map/ppermute | solution.py:17
  217.6 36.6 %all_to_all.8 = bf16[1,8,128,640]{3,2,0,1:T(8,128)(2,1)S(1)} all-to-all(bf16[1,8,128,640]{3,2,0,1:T(8,128)(2,1)S(1)} %bitcast.181), channel_id=1, replica_groups=mesh['video'=4,'frame'=8] {'frame'}, dimensions={1} | all-to-all | bytes 2621440 | tf_op jit(solution)/shard_map/all_to_all | solution.py:132
  260.8 7.1 %copy.62 = bf16[8,128,10,64]{3,0,2,1:T(8,128)(2,1)} copy(bf16[8,128,10,64]{1,0,3,2:T(8,128)(2,1)} %bitcast.185) | data formatting | bytes 2621440 | tf_op jit(solution)/shard_map/reshape;reshape | solution.py:42
  273.3 7.1 %copy.63 = bf16[8,128,10,64]{3,0,2,1:T(8,128)(2,1)} copy(bf16[8,128,10,64]{1,0,3,2:T(8,128)(2,1)} %bitcast.186) | data formatting | bytes 2621440 | tf_op jit(solution)/shard_map/reshape;reshape | solution.py:43
  285.8 7.2 %copy.66 = bf16[8,128,10,64]{3,0,2,1:T(8,128)(2,1)} copy(bf16[8,128,10,64]{1,0,3,2:T(8,128)(2,1)} %bitcast.187) | data formatting | bytes 2621440 | tf_op jit(solution)/shard_map/reshape;reshape | solution.py:44
  293.0 4.6 %multiply_reduce_fusion.2 = (f32[128,10,8]{2,1,0:T(8,128)S(1)}, f32[128,10,8,8]{2,3,1,0:T(8,128)S(1)}) fusion(bf16[8,128,10,64]{3,0,2,1:T(8,128)(2,1)} %copy.62, bf16[8,128,10,64]{3,0,2,1:T(8,128)(2,1)} %copy.63), kind=kOutput, calls=%fused_computation.47 | convolution fusion | flops 10639360 | bytes 2990080 | tf_op jit(solution)/shard_map/fnhd,gnhd->nhfg/dot_general | solution.py:45
  299.8 3.9 %fusion.45 = bf16[8,128,10,64]{3,0,2,1:T(8,128)(2,1)} fusion(f32[8,128,10]{0,2,1:T(8,128)S(1)} %bitcast.200, bf16[8,128,10,64]{3,0,2,1:T(8,128)(2,1)S(1)} %copy-done.4, f32[128,10,8,8]{2,3,1,0:T(8,128)S(1)} %get-tuple-element.167, f32[128,10,8]{2,1,0:T(8,128)S(1)} %get-tuple-element.166), kind=kOutput, calls=%fused_computation.45 | convolution fusion | flops 12042240 | bytes 3031040 | tf_op jit(solution)/shard_map/nhfg,gnhd->nhfd/dot_general | solution.py:52
  303.8 5.1 %copy.67 = bf16[8,128,10,64]{1,3,2,0:T(8,128)(2,1)} copy(bf16[8,128,10,64]{3,0,2,1:T(8,128)(2,1)} %fusion.45) | data formatting | bytes 2621440 | tf_op jit(solution)/shard_map/convert_element_type | solution.py:60
  308.9 34.7 %all_to_all.9 = bf16[8,1,128,640]{2,3,1,0:T(8,128)(2,1)S(1)} all-to-all(bf16[8,1,128,640]{2,3,1,0:T(8,128)(2,1)} %bitcast.188), channel_id=1, replica_groups=mesh['video'=4,'frame'=8] {'frame'}, dimensions={0} | all-to-all | bytes 2621440 | tf_op jit(solution)/shard_map/all_to_all | solution.py:139
  345.0 4.0 %fusion.57 = bf16[1,1024,640]{2,1,0:T(8,128)(2,1)} fusion(bf16[1,1024,640]{2,1,0:T(8,128)(2,1)S(1)} %get-tuple-element.165, bf16[1024,640]{1,0:T(8,128)(2,1)} %bitcast.196, bf16[640,640]{1,0:T(8,128)(2,1)} %param.25), kind=kOutput, calls=%fused_computation.65 | convolution fusion | flops 840826880 | bytes 4751360 | tf_op jit(solution)/shard_map/dot_general | solution.py:140
  (176 shorter events, 136.4 us)
Async XLA Ops:
  6.5 1.1 copy-start
  6.5 5.4 %copy-start.2 = (bf16[1,1024,640]{2,1,0:T(8,128)(2,1)S(1)}, bf16[1,1024,640]{2,1,0:T(8,128)(2,1)}, u32[]{:S(2)}) copy-start(bf16[1,1024,640]{2,1,0:T(8,128)(2,1)} %param.15) | copy-start | bytes 3932164
  6.5 76.5 %all-gather.3.cloned.1.call-start = ((), (), s32[]{:S(2)}) async-start(), calls=%async_computation.2 | async-start | bytes 1474560 | tf_op jit(solution)/shard_map/all_gather | solution.py:90
  9.6 87.3 %all-gather.5.cloned.1.call-start = ((), (), s32[]{:S(2)}) async-start(), calls=%async_computation.3 | async-start | bytes 1474560 | tf_op jit(solution)/shard_map/all_gather | solution.py:91
  12.7 2.6 copy-start.8
  15.3 2.6 copy-start.10
  153.0 2.3 copy-start.3
  153.0 2.3 copy-start.11
  155.3 5.5 %copy-start.9 = (bf16[3,640,640]{2,1,0:T(8,128)(2,1)S(1)}, bf16[3,640,640]{2,1,0:T(8,128)(2,1)}, u32[]{:S(2)}) copy-start(bf16[3,640,640]{2,1,0:T(8,128)(2,1)} %param.21) | copy-start | bytes 7372804
  156.8 57.0 %collective-permute-start = (bf16[1,1024,640]{2,1,0:T(8,128)(2,1)S(1)}, bf16[1,1024,640]{2,1,0:T(8,128)(2,1)S(1)}, u32[]{:S(2)}, u32[]{:S(2)}) collective-permute-start(bf16[1,1024,640]{2,1,0:T(8,128)(2,1)S(1)} %fusion.56), channel_id=1, source_target_pairs={{0,1},{1,2},{2,3},{3,4},{4,5},{5,6},{6,7},{8,9},{9,10},{10,11},{11... | collective-permute-start | bytes 3932168 | tf_op jit(solution)/shard_map/ppermute | solution.py:17
  159.3 55.8 %collective-permute-start.1 = (bf16[1,1024,640]{2,1,0:T(8,128)(2,1)S(1)}, bf16[1,1024,640]{2,1,0:T(8,128)(2,1)S(1)}, u32[]{:S(2)}, u32[]{:S(2)}) collective-permute-start(bf16[1,1024,640]{2,1,0:T(8,128)(2,1)S(1)} %fusion.56), channel_id=1, source_target_pairs={{1,0},{2,1},{3,2},{4,3},{5,4},{6,5},{7,6},{9,8},{10,9},{11,10},{12... | collective-permute-start | bytes 3932168 | tf_op jit(solution)/shard_map/ppermute | solution.py:18
  217.2 38.2 %copy-start.12 = (bf16[640,640]{1,0:T(8,128)(2,1)S(1)}, bf16[640,640]{1,0:T(8,128)(2,1)}, u32[]{:S(2)}) copy-start(bf16[640,640]{1,0:T(8,128)(2,1)} %param.22) | copy-start | bytes 2457604
  254.2 1.1 copy-start.5
  260.8 7.1 %copy-start.6 = (bf16[1,8,128,640]{3,2,0,1:T(8,128)(2,1)S(1)}, bf16[1,8,128,640]{3,2,0,1:T(8,128)(2,1)}, u32[]{:S(2)}) copy-start(bf16[1,8,128,640]{3,2,0,1:T(8,128)(2,1)} %copy-done.5) | copy-start | bytes 3932164
  260.8 7.1 %copy-start.13 = (bf16[640,640]{1,0:T(8,128)(2,1)S(1)}, bf16[640,640]{1,0:T(8,128)(2,1)}, u32[]{:S(2)}) copy-start(bf16[640,640]{1,0:T(8,128)(2,1)} %param.23) | copy-start | bytes 2457604
  273.3 7.1 %copy-start.7 = (bf16[1,8,128,640]{3,2,0,1:T(8,128)(2,1)S(1)}, bf16[1,8,128,640]{3,2,0,1:T(8,128)(2,1)}, u32[]{:S(2)}) copy-start(bf16[1,8,128,640]{3,2,0,1:T(8,128)(2,1)} %copy-done.5) | copy-start | bytes 3932164
  273.3 7.1 %copy-start.14 = (bf16[640,640]{1,0:T(8,128)(2,1)S(1)}, bf16[640,640]{1,0:T(8,128)(2,1)}, u32[]{:S(2)}) copy-start(bf16[640,640]{1,0:T(8,128)(2,1)} %param.24) | copy-start | bytes 2457604
  297.6 2.2 copy-start.4
  345.0 4.0 %copy-start.1 = (bf16[640,640]{1,0:T(8,128)(2,1)S(1)}, bf16[640,640]{1,0:T(8,128)(2,1)}, u32[]{:S(2)}) copy-start(bf16[640,640]{1,0:T(8,128)(2,1)} %param.18) | copy-start | bytes 2457604
Sparse Core Ops, SparseCore 0:
  9.7 44.5 all-gather.2
  56.5 40.3 all-gather.4
where the time goes:
time: 362 us; the launch traced here: 356 us
  matrix products  122 us (34%)
  blocking collectives  71.3 us (20%)
  waiting for transfers between devices  63.1 us (17%)
  local copies, waits for them, and re-layouts  60.4 us (17%)
  other arithmetic  21.1 us (6%)
  between operations  13.9 us (4%)
  starting transfers between devices  4.04 us (1%)
    ppermute x1, waiting for transfers between devices, padded_2(): before = lax.ppermute(last, axis, up)  51.6 us
    all_to_all x1, blocking collectives, per_device(): lax.all_to_all(grouped, 'frame', split_axis=1, concat_axis=0, tiled=True)  36.6 us
    all_to_all x1, blocking collectives, per_device(): lax.all_to_all(mixed, 'frame', split_axis=0, concat_axis=1, tiled=True)  34.7 us
    dot_general x10, matrix products, one_head(): jnp.einsum('fqk,kd->fqd', expo.astype(jnp.bfloat16), va, preferred_elemen...  25.7 us
    dot_general x10, matrix products, local_part(): jnp.einsum('fqk,fkd->fqd', expo.astype(jnp.bfloat16), va, preferred_eleme...  25.4 us
    dot_general x8, matrix products, project(): jnp.dot(rows, weight, preferred_element_type=jnp.float32)  18.9 us
    dot_general x10, matrix products, one_head(): jnp.einsum('fqd,kd->fqk', qa, ka, preferred_element_type=jnp.float32)  16.7 us
    dot_general x10, matrix products, local_part(): jnp.einsum('fqd,fkd->fqk', qa, ka, preferred_element_type=jnp.float32)  16.7 us
  transfers between devices with their start and end apart: 4, of which 2 were waited for; matrix products, arithmetic and copies ran while one was open for 22% of the time, Pallas kernels for 0%

commit v1 on v0

--- a/solution.py
+++ b/solution.py
@@ -136,7 +136,10 @@
     tkeys = project(flat, t_key).reshape(nframes, groups * count, channels)
     tvalues = project(flat, t_value).reshape(nframes, groups * count, channels)
     mixed = temporal_attend(tquery, tkeys, tvalues).reshape(nframes, groups, count, channels)
-    back = lax.all_to_all(mixed, "frame", split_axis=0, concat_axis=1, tiled=True)
+    x_next = jnp.split(mixed, jax.lax.axis_size("frame"), axis=0)
+    r_now = jnp.stack(x_next)
+    arr_now = jax.lax.all_to_all(r_now, axis_name="frame", split_axis=0, concat_axis=0)
+    back = jnp.concatenate(arr_now, axis=1)
     result = second.astype(jnp.float32) + jnp.dot(
         back.reshape(-1, width), t_out, preferred_element_type=jnp.float32
     ).reshape(fdev, pixels, width)

time: 362 us -> 381 us (1.052)
  local copies, waits for them, and re-layouts: 60.4 us -> 79.8 us
    split x0 -> x9, local copies, waits for them, and re-layouts: none -> 16.3 us  [per_device(): x_next = jnp.split(mixed, jax.lax.axis_size('frame'), axis=0)]
    unnamed x33 -> x44, local copies, waits for them, and re-layouts: 6.63 us -> 14.1 us
    convert_element_type x1 -> x0, local copies, waits for them, and re-layouts: 5.1 us -> none  [temporal_attend(): tmixed.transpose(2, 0, 1, 3).reshape(nframes, pixels, width)]
  transfers between devices with their start and end apart: 4 -> 4, of which waited for: 2 -> 2; matrix products, arithmetic and copies ran while one was open for 22% -> 21% of each run, Pallas kernels for 0% -> 0%
where the time goes in v1:
time: 381 us; the launch traced here: 374 us
  matrix products  120 us (31%)
  local copies, waits for them, and re-layouts  79.8 us (21%)
  blocking collectives  71.3 us (19%)
  waiting for transfers between devices  63.3 us (17%)
  other arithmetic  21.1 us (6%)
  between operations  13.9 us (4%)
  starting transfers between devices  4.04 us (1%)
    ppermute x1, waiting for transfers between devices, padded_2(): before = lax.ppermute(last, axis, up)  51.6 us
    all_to_all x1, blocking collectives, per_device(): lax.all_to_all(grouped, 'frame', split_axis=1, concat_axis=0, tiled=True)  36.6 us
    all_to_all x1, blocking collectives, per_device(): jax.lax.all_to_all(r_now, axis_name='frame', split_axis=0, concat_axis=0)  34.7 us
    dot_general x10, matrix products, one_head(): jnp.einsum('fqk,kd->fqd', expo.astype(jnp.bfloat16), va, preferred_elemen...  25.7 us
    dot_general x10, matrix products, local_part(): jnp.einsum('fqk,fkd->fqd', expo.astype(jnp.bfloat16), va, preferred_eleme...  25.4 us
    dot_general x8, matrix products, project(): jnp.dot(rows, weight, preferred_element_type=jnp.float32)  18.9 us
    dot_general x10, matrix products, one_head(): jnp.einsum('fqd,kd->fqk', qa, ka, preferred_element_type=jnp.float32)  16.7 us
    dot_general x10, matrix products, local_part(): jnp.einsum('fqd,fkd->fqk', qa, ka, preferred_element_type=jnp.float32)  16.7 us
  transfers between devices with their start and end apart: 4, of which 2 were waited for; matrix products, arithmetic and copies ran while one was open for 21% of the time, Pallas kernels for 0%

profile of v1, /device:TPU:0, one launch (start us, length us, event | category | flops | bytes accessed | tf_op | source)
XLA Modules:
  0.0 374.4 jit_solution(17548948906862651244)
XLA Ops:
  15.3 2.6 convolution_convert_fusion.3
  20.4 3.5 copy.66
  24.0 3.8 %copy.67 = bf16[1,1024,10,64]{3,1,0,2:T(8,128)(2,1)} copy(bf16[1,1024,10,64]{1,3,2,0:T(8,128)(2,1)} %bitcast.202) | data formatting | bytes 2621440 | tf_op jit(solution)/shard_map/reshape;reshape | solution.py:36
  27.8 3.8 %copy.68 = bf16[1,1024,10,64]{3,1,0,2:T(8,128)(2,1)} copy(bf16[1,1024,10,64]{1,3,2,0:T(8,128)(2,1)} %bitcast.201) | data formatting | bytes 2621440 | tf_op jit(solution)/shard_map/reshape;reshape | solution.py:36
  33.4 49.6 %while.26 = (s32[]{:T(128)}, f32[10,1,1024]{2,1,0:T(1,128)S(1)}, f32[10,1,1024]{2,1,0:T(1,128)S(1)}, f32[10,1,1024,64]{2,3,1,0:T(8,128)}, bf16[10,1,1024,64]{3,2...) while((s32[]{:T(128)}, f32[10,1,1024]{2,1,0:T(1,128)S(1)}, ...), condition=%wide.region_5.6_spmd, body=%wide.region_2.5_spmd.sunk | while | flops 276822016 | bytes 13666393 | solution.py:87
  85.4 11.6 %all-gather.5.cloned.1.call-done = bf16[1024,640]{1,0:T(8,128)(2,1)} async-done(((bf16[128,640]{1,0:T(8,128)(2,1)}), bf16[1024,640]{1,0:T(8,128)(2,1)}) %all-gather.5.cloned.1.call-update) | async-done | bytes 1310736 | tf_op jit(solution)/shard_map/all_gather | solution.py:91
  101.4 51.7 %while.27 = (s32[]{:T(128)}, f32[10,1,1024]{2,0,1:T(8,128)S(1)}, f32[10,1,1024,64]{2,3,1,0:T(8,128)}, f32[10,1,1024]{2,1,0:T(1,128)S(1)}, f32[10,1,1024]{2,1,0:T...) while((s32[]{:T(128)}, f32[10,1,1024]{2,0,1:T(8,128)S(1)}, ...), condition=%wide.region_9.10_spmd, body=%wide.region_6.9_spmd.sunk | while | flops 276959232 | bytes 13707385 | solution.py:108
  108.2 2.6 fusion.120
  118.6 2.6 fusion.120
  123.7 2.6 fusion.120
  128.9 2.6 fusion.120
  134.1 2.6 fusion.120
  139.3 2.6 fusion.120
  144.5 2.6 fusion.120
  162.2 51.6 %collective-permute-done = bf16[1,1024,640]{2,1,0:T(8,128)(2,1)S(1)} collective-permute-done((bf16[1,1024,640]{2,1,0:T(8,128)(2,1)S(1)}, bf16[1,1024,640]{2,1,0:T(8,128)(2,1)S(1)}, u32[]{:S(2)}, u32[]{:S(2)}) %collective-permute-start) | collective-permute-done | bytes 1310752 | tf_op jit(solution)/shard_map/ppermute | solution.py:17
  217.7 36.6 %all_to_all.14 = bf16[1,8,128,640]{3,2,0,1:T(8,128)(2,1)S(1)} all-to-all(bf16[1,8,128,640]{3,2,0,1:T(8,128)(2,1)S(1)} %bitcast.186), channel_id=1, replica_groups=mesh['video'=4,'frame'=8] {'frame'}, dimensions={1} | all-to-all | bytes 2621440 | tf_op jit(solution)/shard_map/all_to_all | solution.py:132
  260.9 7.1 %copy.76 = bf16[8,128,10,64]{3,0,2,1:T(8,128)(2,1)} copy(bf16[8,128,10,64]{1,0,3,2:T(8,128)(2,1)} %bitcast.190) | data formatting | bytes 2621440 | tf_op jit(solution)/shard_map/reshape;reshape | solution.py:42
  273.4 7.1 %copy.77 = bf16[8,128,10,64]{3,0,2,1:T(8,128)(2,1)} copy(bf16[8,128,10,64]{1,0,3,2:T(8,128)(2,1)} %bitcast.191) | data formatting | bytes 2621440 | tf_op jit(solution)/shard_map/reshape;reshape | solution.py:43
  285.9 7.1 %copy.80 = bf16[8,128,10,64]{3,0,2,1:T(8,128)(2,1)} copy(bf16[8,128,10,64]{1,0,3,2:T(8,128)(2,1)} %bitcast.192) | data formatting | bytes 2621440 | tf_op jit(solution)/shard_map/reshape;reshape | solution.py:44
  293.1 4.6 %multiply_reduce_fusion.2 = (f32[128,10,8]{2,1,0:T(8,128)S(1)}, f32[128,10,8,8]{2,3,1,0:T(8,128)S(1)}) fusion(bf16[8,128,10,64]{3,0,2,1:T(8,128)(2,1)} %copy.76, bf16[8,128,10,64]{3,0,2,1:T(8,128)(2,1)} %copy.77), kind=kOutput, calls=%fused_computation.47 | convolution fusion | flops 10639360 | bytes 2990080 | tf_op jit(solution)/shard_map/fnhd,gnhd->nhfg/dot_general | solution.py:45
  299.9 2.9 fusion.45
  302.8 5.4 %fusion.84 = (bf16[1,128,10,64]{3,0,2,1:T(2,128)(2,1)S(1)}, bf16[1,128,10,64]{3,0,2,1:T(2,128)(2,1)S(1)}, bf16[1,128,10,64]{3,0,2,1:T(2,128)(2,1)S(1)}, bf16[1,1...) fusion(bf16[8,128,10,64]{3,0,2,1:T(8,128)(2,1)S(1)} %fusion.45), kind=kLoop, calls=%fused_computation.106 | loop fusion | bytes 2621440 | tf_op jit(solution)/shard_map/split | solution.py:139
  327.3 34.7 %all_to_all.15 = bf16[8,1,1,128,640]{3,4,2,1,0:T(8,128)(2,1)S(1)} all-to-all(bf16[8,1,1,128,640]{3,4,2,1,0:T(8,128)(2,1)} %constant_dynamic-update-slice_fusion.2), channel_id=1, replica_groups=mesh['video'=4,'frame'=8] {'frame'}, dimensions={0} | all-to-all | bytes 2621440 | tf_op jit(solution)/shard_map/all_to_all | solution.py:141
  363.4 4.0 %fusion.57 = bf16[1,1024,640]{2,1,0:T(8,128)(2,1)} fusion(bf16[1,1024,640]{2,1,0:T(8,128)(2,1)S(1)} %get-tuple-element.173, bf16[1024,640]{1,0:T(8,128)(2,1)} %bitcast.200, bf16[640,640]{1,0:T(8,128)(2,1)} %param.25), kind=kOutput, calls=%fused_computation.65 | convolution fusion | flops 840826880 | bytes 4751360 | tf_op jit(solution)/shard_map/dot_general | solution.py:143
  (196 shorter events, 155.3 us)
Async XLA Ops:
  6.5 1.1 copy-start
  6.5 5.3 %copy-start.2 = (bf16[1,1024,640]{2,1,0:T(8,128)(2,1)S(1)}, bf16[1,1024,640]{2,1,0:T(8,128)(2,1)}, u32[]{:S(2)}) copy-start(bf16[1,1024,640]{2,1,0:T(8,128)(2,1)} %param.15) | copy-start | bytes 3932164
  6.5 76.5 %all-gather.3.cloned.1.call-start = ((), (), s32[]{:S(2)}) async-start(), calls=%async_computation.2 | async-start | bytes 1474560 | tf_op jit(solution)/shard_map/all_gather | solution.py:90
  9.6 87.5 %all-gather.5.cloned.1.call-start = ((), (), s32[]{:S(2)}) async-start(), calls=%async_computation.3 | async-start | bytes 1474560 | tf_op jit(solution)/shard_map/all_gather | solution.py:91
  12.7 2.5 copy-start.8
  15.3 2.6 copy-start.12
  153.1 2.3 copy-start.3
  153.1 2.3 copy-start.13
  155.4 5.5 %copy-start.11 = (bf16[3,640,640]{2,1,0:T(8,128)(2,1)S(1)}, bf16[3,640,640]{2,1,0:T(8,128)(2,1)}, u32[]{:S(2)}) copy-start(bf16[3,640,640]{2,1,0:T(8,128)(2,1)} %param.21) | copy-start | bytes 7372804
  156.9 57.0 %collective-permute-start = (bf16[1,1024,640]{2,1,0:T(8,128)(2,1)S(1)}, bf16[1,1024,640]{2,1,0:T(8,128)(2,1)S(1)}, u32[]{:S(2)}, u32[]{:S(2)}) collective-permute-start(bf16[1,1024,640]{2,1,0:T(8,128)(2,1)S(1)} %fusion.56), channel_id=1, source_target_pairs={{0,1},{1,2},{2,3},{3,4},{4,5},{5,6},{6,7},{8,9},{9,10},{10,11},{11... | collective-permute-start | bytes 3932168 | tf_op jit(solution)/shard_map/ppermute | solution.py:17
  159.4 55.8 %collective-permute-start.1 = (bf16[1,1024,640]{2,1,0:T(8,128)(2,1)S(1)}, bf16[1,1024,640]{2,1,0:T(8,128)(2,1)S(1)}, u32[]{:S(2)}, u32[]{:S(2)}) collective-permute-start(bf16[1,1024,640]{2,1,0:T(8,128)(2,1)S(1)} %fusion.56), channel_id=1, source_target_pairs={{1,0},{2,1},{3,2},{4,3},{5,4},{6,5},{7,6},{9,8},{10,9},{11,10},{12... | collective-permute-start | bytes 3932168 | tf_op jit(solution)/shard_map/ppermute | solution.py:18
  217.3 38.2 %copy-start.14 = (bf16[640,640]{1,0:T(8,128)(2,1)S(1)}, bf16[640,640]{1,0:T(8,128)(2,1)}, u32[]{:S(2)}) copy-start(bf16[640,640]{1,0:T(8,128)(2,1)} %param.22) | copy-start | bytes 2457604
  254.3 1.1 copy-start.5
  260.9 7.1 %copy-start.6 = (bf16[1,8,128,640]{3,2,0,1:T(8,128)(2,1)S(1)}, bf16[1,8,128,640]{3,2,0,1:T(8,128)(2,1)}, u32[]{:S(2)}) copy-start(bf16[1,8,128,640]{3,2,0,1:T(8,128)(2,1)} %copy-done.5) | copy-start | bytes 3932164
  260.9 7.1 %copy-start.15 = (bf16[640,640]{1,0:T(8,128)(2,1)S(1)}, bf16[640,640]{1,0:T(8,128)(2,1)}, u32[]{:S(2)}) copy-start(bf16[640,640]{1,0:T(8,128)(2,1)} %param.23) | copy-start | bytes 2457604
  273.4 7.1 %copy-start.7 = (bf16[1,8,128,640]{3,2,0,1:T(8,128)(2,1)S(1)}, bf16[1,8,128,640]{3,2,0,1:T(8,128)(2,1)}, u32[]{:S(2)}) copy-start(bf16[1,8,128,640]{3,2,0,1:T(8,128)(2,1)} %copy-done.5) | copy-start | bytes 3932164
  273.4 7.1 %copy-start.16 = (bf16[640,640]{1,0:T(8,128)(2,1)S(1)}, bf16[640,640]{1,0:T(8,128)(2,1)}, u32[]{:S(2)}) copy-start(bf16[640,640]{1,0:T(8,128)(2,1)} %param.24) | copy-start | bytes 2457604
  297.7 2.2 copy-start.4
  318.8 5.7 %copy-start.10 = (bf16[1,128,10,64]{1,3,2,0:T(8,128)(2,1)S(1)}, bf16[1,128,10,64]{1,3,2,0:T(8,128)(2,1)}, u32[]{:S(2)}) copy-start(bf16[1,128,10,64]{1,3,2,0:T(8,128)(2,1)} %copy.85) | copy-start | bytes 491524
  318.8 6.4 %copy-start.9 = (bf16[1,128,10,64]{1,3,2,0:T(8,128)(2,1)S(1)}, bf16[1,128,10,64]{1,3,2,0:T(8,128)(2,1)}, u32[]{:S(2)}) copy-start(bf16[1,128,10,64]{1,3,2,0:T(8,128)(2,1)} %copy.86) | copy-start | bytes 491524
  363.4 4.0 %copy-start.1 = (bf16[640,640]{1,0:T(8,128)(2,1)S(1)}, bf16[640,640]{1,0:T(8,128)(2,1)}, u32[]{:S(2)}) copy-start(bf16[640,640]{1,0:T(8,128)(2,1)} %param.18) | copy-start | bytes 2457604
Sparse Core Ops, SparseCore 0:
  9.7 44.5 all-gather.2
  56.5 40.5 all-gather.4
